TPU v7x, 32 devices: a whole 2x2x4 slice. The times are simulated.
32 devices in a mesh: row: 4 (over y, core), col: 8 (over z, x).
Axes of the slice: x: 2, y: 2, z: 4, core: 2. Of those that a mesh axis runs over, the one named last changes fastest.
Arguments:
- weight: bfloat16 [8192, 16384], P('row', 'col'), may hold values from -3 to 3
- momentum: float32 [8192, 16384], P('row', 'col'), may hold values from -100 to 100, as said below
- gradient: bfloat16 [8192, 16384], P('row', 'col'), may hold values from -6 to 6
- prev_basis: bfloat16 [16384, 512], P('col'), may hold values from -6 to 6
Outputs:
- new_weight: bfloat16 [8192, 16384], P('row', 'col')
- new_momentum: float32 [8192, 16384], P('row', 'col')
- new_basis: bfloat16 [16384, 512], P('col')
Inputs may be any that keep to these rules, and one draw needn't show every extreme that they name: momentum has rows and columns of different scales.
All inputs are finite; a program needn't handle non-finite values.
Results may differ from a plain program's by a relative error of at most 0.0021.
Values may be sent and summed in bfloat16 or wider, within the bound.
No kernel may reach another device: no remote copies, remote signals or barrier semaphores. Data moves between devices by JAX's collectives and lax.ppermute only.
A program may use at most 128 MiB of HBM per device.

v0:
```python
import jax
import jax.numpy as jnp
from jax import lax
from jax.sharding import PartitionSpec as P

M = 8192
N = 16384
decay_loss = 0.1
step_size = 0.4
epsilon = 1e-06


def orthogonalize(left_factor, gram_matrix):
    lower_tri = jnp.linalg.cholesky(gram_matrix)
    return jax.scipy.linalg.solve_triangular(lower_tri, left_factor.T, lower=True).T


def per_device(weight, momentum, gradient, prev_basis):
    high = lax.Precision.HIGHEST
    buffer = momentum + gradient.astype(jnp.float32)
    partial_left = jnp.dot(buffer, prev_basis.astype(jnp.float32), precision=high)
    left_factor = lax.psum(partial_left, "col")
    gram_matrix = lax.psum(jnp.dot(left_factor.T, left_factor, precision=high), "row")
    orthonormal = orthogonalize(left_factor, gram_matrix)
    right_piece = lax.psum_scatter(
        jnp.dot(buffer.T, orthonormal, precision=high), "row", scatter_dimension=0, tiled=True
    )
    square_sum = lax.psum(jnp.sum(right_piece * right_piece, axis=0), ("row", "col"))
    column_scale = jnp.sqrt(square_sum / N + epsilon)
    basis_piece = (right_piece / column_scale).astype(jnp.bfloat16)
    new_basis = lax.all_gather(basis_piece, "row", axis=0, tiled=True)
    basis_float = new_basis.astype(jnp.float32)
    new_momentum = buffer - decay_loss * jnp.dot(
        orthonormal * column_scale, basis_float.T, precision=high
    )
    update = jnp.dot(orthonormal, basis_float.T, precision=high)
    new_weight = (weight.astype(jnp.float32) - step_size * (M / N) ** 0.5 * update).astype(
        jnp.bfloat16
    )
    return (new_weight, new_momentum, new_basis)


def solution(mesh):
    return jax.shard_map(
        per_device,
        mesh=mesh,
        in_specs=(P("row", "col"), P("row", "col"), P("row", "col"), P("col", None)),
        out_specs=(P("row", "col"), P("row", "col"), P("col", None)),
        check_vma=False,
    )
```

profile of v0, /device:TPU:0, one launch (start us, length us, event | category | flops | bytes accessed | tf_op | source)
XLA Modules:
  0.0 632.8 jit_solution(8107940526218711960)
XLA Ops:
  7.2 1.5 copy-done
  8.8 18.2 %fusion.1 = f32[2048,512]{1,0:T(8,128)} fusion(bf16[2048,512]{1,0:T(8,128)(2,1)S(1)} %copy-done, f32[2048,2048]{1,0:T(8,128)} %param.5, bf16[2048,2048]{1,0:T(8,128)(2,1)} %param.6), kind=kOutput, calls=%fused_computation.6 | convolution fusion | flops 25778192384 | bytes 31457280 | tf_op jit(solution)/shard_map/dot_general | solution.py:21
  27.0 159.2 %all-reduce.4.cloned.1.call-done = f32[2048,512]{1,0:T(8,128)} async-done(((f32[2048,512]{1,0:T(8,128)}), f32[2048,512]{1,0:T(8,128)}) %all-reduce.4.cloned.1.call-update) | async-done | bytes 4194320 | tf_op jit(solution)/shard_map/psum | solution.py:22
  186.2 11.4 %fusion.42 = f32[512,512]{0,1:T(8,128)} fusion(f32[2048,512]{1,0:T(8,128)} %all-reduce.4.cloned.1.call-done), kind=kOutput, calls=%fused_computation.81 | convolution fusion | flops 6442450944 | bytes 5242880 | tf_op jit(solution)/shard_map/dot_general | solution.py:23
  197.9 35.2 %all-reduce.6.cloned.1.call-done = f32[512,512]{0,1:T(8,128)} async-done(((f32[512,512]{0,1:T(8,128)}), f32[512,512]{0,1:T(8,128)}) %all-reduce.6.cloned.1.call-update) | async-done | bytes 1048592 | tf_op jit(solution)/shard_map/psum | solution.py:23
  233.1 1.6 copy.8
  234.7 1.4 fusion.18
  236.1 11.7 %cholesky.104 = f32[128,128]{1,0:T(8,128)S(1)} custom-call(f32[128,128]{1,0:T(8,128)S(1)} %cholesky.266), custom_call_target="Cholesky" | custom-call | tf_op jit(solution)/shard_map/jit(cholesky)/cholesky | solution.py:14
  247.9 9.8 %custom-call.31 = f32[1,128,128]{1,2,0:T(8,128)S(1)} custom-call(f32[1,128,128]{2,1,0:T(8,128)S(1)} %get-tuple-element.30), custom_call_target="InvertDiagBlocksLowerTriangular" | custom-call | tf_op jit(solution)/shard_map/jit(cholesky)/cholesky | solution.py:14
  257.8 0.3 constant_dynamic-update-slice_fusion.3
  258.1 0.3 convolution_subtract_fusion.2
  258.5 11.7 %cholesky.217 = f32[128,128]{1,0:T(8,128)S(1)} custom-call(f32[128,128]{1,0:T(8,128)S(1)} %cholesky.270), custom_call_target="Cholesky" | custom-call | tf_op jit(solution)/shard_map/jit(cholesky)/cholesky | solution.py:14
  270.2 10.2 %custom-call.32 = f32[1,128,128]{1,2,0:T(8,128)S(1)} custom-call(f32[1,128,128]{2,1,0:T(8,128)S(1)} %get-tuple-element.27), custom_call_target="InvertDiagBlocksLowerTriangular" | custom-call | tf_op jit(solution)/shard_map/jit(cholesky)/cholesky | solution.py:14
  280.7 0.4 convolution_subtract_fusion.3
  281.1 11.7 %cholesky.238 = f32[128,128]{1,0:T(8,128)S(1)} custom-call(f32[128,128]{1,0:T(8,128)S(1)} %cholesky.275), custom_call_target="Cholesky" | custom-call | tf_op jit(solution)/shard_map/jit(cholesky)/cholesky | solution.py:14
  292.9 0.6 compare_reduce_fusion.1
  293.5 9.8 %custom-call.33 = f32[1,128,128]{1,2,0:T(8,128)S(1)} custom-call(f32[1,128,128]{2,1,0:T(8,128)S(1)} %get-tuple-element.24), custom_call_target="InvertDiagBlocksLowerTriangular" | custom-call | tf_op jit(solution)/shard_map/jit(cholesky)/cholesky | solution.py:14
  303.5 0.4 convolution_subtract_fusion.4
  303.9 11.7 %cholesky.255 = f32[128,128]{1,0:T(8,128)S(1)} custom-call(f32[128,128]{1,0:T(8,128)S(1)} %convolution_subtract_fusion.4), custom_call_target="Cholesky" | custom-call | tf_op jit(solution)/shard_map/jit(cholesky)/cholesky | solution.py:14
  315.7 0.7 compare_reduce_fusion
  316.3 0.6 compare_reduce_fusion.2
  319.8 8.0 %while.1 = (s32[]{:T(128)}, f32[512,512]{1,0:T(8,128)S(1)}, s32[4,2]{0,1:T(2,128)S(1)}, f32[4,128,128]{2,1,0:T(8,128)S(1)}, s32[]{:T(128)}) while((s32[]{:T(128)}, f32[512,512]{1,0:T(8,128)S(1)}, s32[4,2]{0,1:T(2,128)S(1)}, f32[4,128,128]{2,1,0:T(8,128)S(1)}, s32[]{:T(128)}) %tuple.31), condition=%wide.while_cond, body=%wide.while_body.sunk | while | flops 2 | bytes 131181 | solution.py:15
  319.9 0.5 fusion.54
  320.4 1.4 bitcast_dynamic-update-slice_fusion.2
  321.9 0.5 fusion.54
  322.4 1.4 bitcast_dynamic-update-slice_fusion.2
  323.9 0.5 fusion.54
  324.4 1.4 bitcast_dynamic-update-slice_fusion.2
  325.9 0.5 fusion.54
  326.4 1.4 bitcast_dynamic-update-slice_fusion.2
  327.9 39.3 %custom-call.34 = f32[4,128,128]{1,2,0:T(8,128)S(1)} custom-call(f32[4,128,128]{2,1,0:T(8,128)S(1)} %get-tuple-element.10), custom_call_target="InvertDiagBlocksLowerTriangular" | custom-call | tf_op jit(solution)/shard_map/jit(_solve_triangular)/triangular_solve | solution.py:15
  367.2 2.4 fusion.16
  369.6 3.1 convolution_subtract_fusion.1
  372.7 1.1 fusion.30
  373.8 5.0 convolution_subtract_fusion
  378.8 1.1 fusion.28
  379.9 7.2 %fusion.9 = f32[128,2048]{0,1:T(8,128)S(1)} fusion(f32[128,2048]{1,0:T(8,128)S(1)} %fusion.28, f32[128,2048]{1,0:T(8,128)S(1)} %fusion.30, f32[128,2048]{1,0:T(8,128)S(1)} %fusion.16, f32[512,2048]{0,1:T(8,128)S(1)} %bitcast.57, f32[512,512]{1,0:T(8,128)} %copy-done.7), kind=kOutput, calls=%fused_computation.15 | convolution fusion | flops 1209794560 | bytes 5439488 | tf_op jit(solution)/shard_map/jit(_solve_triangular)/triangular_solve | solution.py:15
  387.1 1.1 fusion.27
  388.2 1.0 copy-done.6
  389.2 56.3 %fusion = f32[2048,512]{1,0:T(8,128)} fusion(f32[2048,2048]{1,0:T(8,128)} %param.5, bf16[2048,2048]{1,0:T(8,128)(2,1)S(1)} %bitcast.59, f32[128,2048]{1,0:T(8,128)S(1)} %fusion.27, f32[128,2048]{1,0:T(8,128)S(1)} %fusion.28, f32[128,2048]{1,0:T(8,128)S(1)} %fusion.30, f32[128,2048]{1,0:T(8,128)S(1)} %fusion.16), kind=kOutput, calls=%fused_computation.5 | convolution fusion | flops 25781338112 | bytes 33554432 | tf_op jit(solution)/shard_map/dot_general | solution.py:26
  445.6 45.2 %reduce-scatter.2.cloned.1.call-done = f32[512,512]{1,0:T(8,128)} async-done(((f32[2048,512]{1,0:T(8,128)}), f32[512,512]{1,0:T(8,128)}) %reduce-scatter.2.cloned.1.call-update) | async-done | bytes 1048592 | tf_op jit(solution)/shard_map/reduce_scatter | solution.py:25
  490.8 1.3 multiply_reduce_fusion
  492.1 39.3 %psum.23 = f32[512]{0:T(512)S(1)} all-reduce(f32[512]{0:T(512)S(1)} %multiply_reduce_fusion), channel_id=1, replica_groups=mesh['row'=4,'col'=8] {'row','col'}, use_global_device_ids=true, to_apply=%region_12.13 | all-reduce | flops 512 | bytes 4096 | tf_op jit(solution)/shard_map/psum | solution.py:28
  531.4 2.1 divide_convert_fusion
  533.6 23.5 %all-gather.2.cloned.1.call-done = bf16[2048,512]{1,0:T(8,128)(2,1)} async-done(((bf16[512,512]{1,0:T(8,128)(2,1)}), bf16[2048,512]{1,0:T(8,128)(2,1)}) %all-gather.2.cloned.1.call-update) | async-done | bytes 2097168 | tf_op jit(solution)/shard_map/all_gather | solution.py:31
  557.1 35.6 %multiply_subtract_fusion = f32[2048,2048]{1,0:T(8,128)} fusion(bf16[2048,512]{1,0:T(8,128)(2,1)} %all-gather.2.cloned.1.call-done, f32[2048,2048]{1,0:T(8,128)} %param.5, bf16[2048,2048]{1,0:T(8,128)(2,1)} %param.6, f32[512]{0:T(512)S(1)} %add_sqrt_fusion, f32[128,2048]{1,0:T(8,128)} %copy-done.6, f32[128,2048]{1,0:T(8,128)S(1)} %fusion.28, ...), kind=kOutput, calls=%fused_computation.2 | convolution fusion | flops 25790775296 | bytes 48236544 | tf_op jit(solution)/shard_map/dot_general | solution.py:33
  592.7 32.0 %subtract_convert_fusion = bf16[2048,2048]{1,0:T(8,128)(2,1)} fusion(bf16[2048,2048]{1,0:T(8,128)(2,1)} %param.4, bf16[2048,512]{1,0:T(8,128)(2,1)} %all-gather.2.cloned.1.call-done, f32[128,2048]{1,0:T(8,128)} %copy-done.6, f32[128,2048]{1,0:T(8,128)} %copy-done.4, f32[128,2048]{1,0:T(8,128)} %copy-done.3, f32[128,2048]{1,0:T(8,128)S(1)} %fusion.16), kind=kOutput, calls=%fused_computation.3 | convolution fusion | flops 25789726720 | bytes 23068672 | tf_op jit(solution)/shard_map/dot_general | solution.py:36
  624.7 1.3 copy.28
  (46 shorter events, 1.8 us)
Async XLA Ops:
  7.2 1.6 copy-start
  7.2 179.1 %all-reduce.4.cloned.1.call-start = ((), (), s32[]{:S(2)}) async-start(), calls=%async_computation.1 | async-start | bytes 8388608 | tf_op jit(solution)/shard_map/psum | solution.py:22
  27.0 206.1 %all-reduce.6.cloned.1.call-start = ((), (), s32[]{:S(2)}) async-start(), calls=%async_computation.2 | async-start | bytes 2097152 | tf_op jit(solution)/shard_map/psum | solution.py:23
  197.7 293.1 %reduce-scatter.2.cloned.1.call-start = ((), (), s32[]{:S(2)}) async-start(), calls=%async_computation.3 | async-start | bytes 5242880 | tf_op jit(solution)/shard_map/reduce_scatter | solution.py:25
  327.8 39.3 %copy-start.7 = (f32[512,512]{1,0:T(8,128)}, f32[512,512]{1,0:T(8,128)S(1)}, u32[]{:S(2)}) copy-start(f32[512,512]{1,0:T(8,128)S(1)} %get-tuple-element.99) | copy-start | bytes 3145732
  367.2 6.6 %copy-start.2 = (f32[2048,512]{1,0:T(8,128)S(1)}, f32[2048,512]{1,0:T(8,128)}, u32[]{:S(2)}) copy-start(f32[2048,512]{1,0:T(8,128)} %all-reduce.4.cloned.1.call-done) | copy-start | bytes 12582916
  372.7 16.5 %slice-start = ((s8[8388608]{0:T(1024)(128)(4,1)}), s8[4194304]{0:T(1024)(128)(4,1)S(1)}, s32[]{:S(2)}) async-start(s8[8388608]{0:T(1024)(128)(4,1)} %bitcast.58), calls=%async_computation.5 | async-start | bytes 8388608
  373.8 183.2 %copy-start.3 = (f32[128,2048]{1,0:T(8,128)}, f32[128,2048]{1,0:T(8,128)S(1)}, u32[]{:S(2)}) copy-start(f32[128,2048]{1,0:T(8,128)S(1)} %fusion.30) | copy-start | bytes 3145732
  378.8 10.4 %slice-start.1 = ((s8[8388608]{0:T(1024)(128)(4,1)}), s8[4194304]{0:T(1024)(128)(4,1)S(1)}, s32[]{:S(2)}) async-start(s8[8388608]{0:T(1024)(128)(4,1)} %bitcast.58), calls=%async_computation.6 | async-start | bytes 8388608
  379.9 177.2 %copy-start.4 = (f32[128,2048]{1,0:T(8,128)}, f32[128,2048]{1,0:T(8,128)S(1)}, u32[]{:S(2)}) copy-start(f32[128,2048]{1,0:T(8,128)S(1)} %fusion.28) | copy-start | bytes 3145732
  388.2 1.0 copy-start.6
  445.6 111.5 %all-gather.2.cloned.1.call-start = ((), (), s32[]{:S(2)}) async-start(), calls=%async_computation.4 | async-start | bytes 2621440 | tf_op jit(solution)/shard_map/all_gather | solution.py:31
  592.7 32.1 %copy-start.5 = (bf16[2048,512]{1,0:T(8,128)(2,1)S(1)}, bf16[2048,512]{1,0:T(8,128)(2,1)}, u32[]{:S(2)}) copy-start(bf16[2048,512]{1,0:T(8,128)(2,1)} %all-gather.2.cloned.1.call-done) | copy-start | bytes 6291460
  592.7 33.4 %copy-start.1 = (bf16[2048,512]{1,0:T(8,128)(2,1)S(1)}, bf16[2048,512]{1,0:T(8,128)(2,1)}, u32[]{:S(2)}) copy-start(bf16[2048,512]{1,0:T(8,128)(2,1)} %param.7) | copy-start | bytes 6291460
Sparse Core Ops, SparseCore 0:
  27.1 159.1 all-reduce.3
  197.8 35.2 all-reduce.5
  445.7 45.0 reduce-scatter.1
  533.7 23.3 all-gather.1
where the time goes:
time: 639 us; the launch traced here: 633 us
  waiting for transfers between devices  263 us (41%)
  matrix products  176 us (28%)
  other arithmetic  123 us (19%)
  blocking collectives  39.3 us (6%)
  between operations  16.8 us (3%)
  local copies, waits for them, and re-layouts  13.5 us (2%)
    psum x1, waiting for transfers between devices, per_device(): left_factor = lax.psum(partial_left, 'col')  159 us
    another operation x14, other arithmetic, orthogonalize(): lower_tri = jnp.linalg.cholesky(gram_matrix)  78.8 us
    dot_general x1, matrix products, per_device(): jnp.dot(buffer.T, orthonormal, precision=high)  56.3 us
    reduce_scatter x1, waiting for transfers between devices, per_device(): lax.psum_scatter(jnp.dot(buffer.T, orthonormal, precision=high), 'row', s...  45.2 us
    another operation x3, other arithmetic, orthogonalize(): jax.scipy.linalg.solve_triangular(lower_tri, left_factor.T, lower=True)  39.6 us
    psum x1, blocking collectives, per_device(): lax.psum(jnp.sum(right_piece * right_piece, axis=0), ('row', 'col'))  39.3 us
    dot_general x1, matrix products, per_device(): jnp.dot(orthonormal * column_scale, basis_float.T, precision=high)  35.6 us
    psum x1, waiting for transfers between devices, per_device(): lax.psum(jnp.dot(left_factor.T, left_factor, precision=high), 'row')  35.2 us
  transfers between devices with their start and end apart: 4, of which 4 were waited for; matrix products, arithmetic and copies ran while one was open for 0% of the time, Pallas kernels for 0%

commit v1 on v0

--- a/solution.py
+++ b/solution.py
@@ -19,7 +19,11 @@
     high = lax.Precision.HIGHEST
     buffer = momentum + gradient.astype(jnp.float32)
     partial_left = jnp.dot(buffer, prev_basis.astype(jnp.float32), precision=high)
-    left_factor = lax.psum(partial_left, "col")
+    left_factor = partial_left
+    for hop in (1, 2, 4):
+        left_factor = left_factor + lax.ppermute(
+            left_factor, "col", [(dev, dev ^ hop) for dev in range(8)]
+        )
     gram_matrix = lax.psum(jnp.dot(left_factor.T, left_factor, precision=high), "row")
     orthonormal = orthogonalize(left_factor, gram_matrix)
     right_piece = lax.psum_scatter(

time: 639 us -> 855 us (1.34)
  waiting for transfers between devices: 263 us -> 459 us
  other arithmetic: 123 us -> 134 us
    ppermute x0 -> x3, waiting for transfers between devices: none -> 360 us  [per_device(): lax.ppermute(left_factor, 'col', [(dev, dev ^ hop) for dev in range(8)])]
    psum x1 -> x0, waiting for transfers between devices: 159 us -> none  [per_device(): left_factor = lax.psum(partial_left, 'col')]
  transfers between devices with their start and end apart: 4 -> 6, of which waited for: 4 -> 6; matrix products, arithmetic and copies ran while one was open for 0% -> 1% of each run, Pallas kernels for 0% -> 0%
where the time goes in v1:
time: 855 us; the launch traced here: 848 us
  waiting for transfers between devices  459 us (54%)
  matrix products  176 us (21%)
  other arithmetic  134 us (16%)
  blocking collectives  39.2 us (5%)
  between operations  17 us (2%)
  local copies, waits for them, and re-layouts  14 us (2%)
    ppermute x3, waiting for transfers between devices, per_device(): lax.ppermute(left_factor, 'col', [(dev, dev ^ hop) for dev in range(8)])  360 us
    another operation x14, other arithmetic, orthogonalize(): lower_tri = jnp.linalg.cholesky(gram_matrix)  79 us
    dot_general x1, matrix products, per_device(): jnp.dot(buffer.T, orthonormal, precision=high)  56.3 us
    reduce_scatter x1, waiting for transfers between devices, per_device(): lax.psum_scatter(jnp.dot(buffer.T, orthonormal, precision=high), 'row', s...  45.2 us
    another operation x3, other arithmetic, orthogonalize(): jax.scipy.linalg.solve_triangular(lower_tri, left_factor.T, lower=True)  39.4 us
    psum x1, blocking collectives, per_device(): lax.psum(jnp.sum(right_piece * right_piece, axis=0), ('row', 'col'))  39.2 us
    dot_general x1, matrix products, per_device(): jnp.dot(orthonormal * column_scale, basis_float.T, precision=high)  35.6 us
    dot_general x1, matrix products, per_device(): update = jnp.dot(orthonormal, basis_float.T, precision=high)  32 us
  transfers between devices with their start and end apart: 6, of which 6 were waited for; matrix products, arithmetic and copies ran while one was open for 1% of the time, Pallas kernels for 0%

profile of v1, /device:TPU:0, one launch (start us, length us, event | category | flops | bytes accessed | tf_op | source)
XLA Modules:
  0.0 847.6 jit_solution(10008172545762618687)
XLA Ops:
  7.2 1.5 copy-done
  8.8 16.6 %fusion.1 = f32[2048,512]{1,0:T(8,128)S(1)} fusion(bf16[2048,512]{1,0:T(8,128)(2,1)S(1)} %copy-done, f32[2048,2048]{1,0:T(8,128)} %param.5, bf16[2048,2048]{1,0:T(8,128)(2,1)} %param.6), kind=kOutput, calls=%fused_computation.6 | convolution fusion | flops 25778192384 | bytes 31457280 | tf_op jit(solution)/shard_map/dot_general | solution.py:21
  25.4 3.0 collective-permute-start
  28.4 90.6 %collective-permute-done = f32[2048,512]{1,0:T(8,128)S(1)} collective-permute-done((f32[2048,512]{1,0:T(8,128)S(1)}, f32[2048,512]{1,0:T(8,128)S(1)}, u32[]{:S(2)}, u32[]{:S(2)}) %collective-permute-start) | collective-permute-done | bytes 4194336 | tf_op jit(solution)/shard_map/ppermute | solution.py:24
  119.0 1.0 add.66
  120.0 1.9 collective-permute-start.1
  121.9 89.9 %collective-permute-done.1 = f32[2048,512]{1,0:T(8,128)S(1)} collective-permute-done((f32[2048,512]{1,0:T(8,128)S(1)}, f32[2048,512]{1,0:T(8,128)S(1)}, u32[]{:S(2)}, u32[]{:S(2)}) %collective-permute-start.1) | collective-permute-done | bytes 4194336 | tf_op jit(solution)/shard_map/ppermute | solution.py:24
  211.8 3.0 add.67
  214.8 2.6 collective-permute-start.2
  217.4 179.4 %collective-permute-done.2 = f32[2048,512]{1,0:T(8,128)} collective-permute-done((f32[2048,512]{1,0:T(8,128)}, f32[2048,512]{1,0:T(8,128)}, u32[]{:S(2)}, u32[]{:S(2)}) %collective-permute-start.2) | collective-permute-done | bytes 4194336 | tf_op jit(solution)/shard_map/ppermute | solution.py:24
  396.8 13.5 %fusion.14 = f32[512,512]{0,1:T(8,128)} fusion(f32[2048,512]{1,0:T(8,128)} %add.67, f32[2048,512]{1,0:T(8,128)} %collective-permute-done.2), kind=kOutput, calls=%fused_computation.21 | convolution fusion | flops 6443499520 | bytes 9437184 | tf_op jit(solution)/shard_map/dot_general | solution.py:27
  410.6 6.5 add_bitcast_fusion
  417.1 30.5 %all-reduce.3.cloned.1.call-done = f32[512,512]{0,1:T(8,128)} async-done(((f32[512,512]{0,1:T(8,128)}), f32[512,512]{0,1:T(8,128)}) %all-reduce.3.cloned.1.call-update) | async-done | bytes 1048592 | tf_op jit(solution)/shard_map/psum | solution.py:27
  447.6 1.6 copy.8
  449.2 1.4 fusion.21
  450.7 11.7 %cholesky.104 = f32[128,128]{1,0:T(8,128)S(1)} custom-call(f32[128,128]{1,0:T(8,128)S(1)} %cholesky.266), custom_call_target="Cholesky" | custom-call | tf_op jit(solution)/shard_map/jit(cholesky)/cholesky | solution.py:14
  462.4 9.8 %custom-call.31 = f32[1,128,128]{1,2,0:T(8,128)S(1)} custom-call(f32[1,128,128]{2,1,0:T(8,128)S(1)} %get-tuple-element.30), custom_call_target="InvertDiagBlocksLowerTriangular" | custom-call | tf_op jit(solution)/shard_map/jit(cholesky)/cholesky | solution.py:14
  473.0 11.7 %cholesky.217 = f32[128,128]{1,0:T(8,128)S(1)} custom-call(f32[128,128]{1,0:T(8,128)S(1)} %cholesky.270), custom_call_target="Cholesky" | custom-call | tf_op jit(solution)/shard_map/jit(cholesky)/cholesky | solution.py:14
  484.8 10.3 %custom-call.32 = f32[1,128,128]{1,2,0:T(8,128)S(1)} custom-call(f32[1,128,128]{2,1,0:T(8,128)S(1)} %get-tuple-element.27), custom_call_target="InvertDiagBlocksLowerTriangular" | custom-call | tf_op jit(solution)/shard_map/jit(cholesky)/cholesky | solution.py:14
  495.7 11.7 %cholesky.238 = f32[128,128]{1,0:T(8,128)S(1)} custom-call(f32[128,128]{1,0:T(8,128)S(1)} %cholesky.275), custom_call_target="Cholesky" | custom-call | tf_op jit(solution)/shard_map/jit(cholesky)/cholesky | solution.py:14
  507.5 0.7 compare_reduce_fusion.1
  508.2 9.8 %custom-call.33 = f32[1,128,128]{1,2,0:T(8,128)S(1)} custom-call(f32[1,128,128]{2,1,0:T(8,128)S(1)} %get-tuple-element.24), custom_call_target="InvertDiagBlocksLowerTriangular" | custom-call | tf_op jit(solution)/shard_map/jit(cholesky)/cholesky | solution.py:14
  518.6 11.9 %cholesky.255 = f32[128,128]{1,0:T(8,128)S(1)} custom-call(f32[128,128]{1,0:T(8,128)S(1)} %convolution_subtract_fusion.2), custom_call_target="Cholesky" | custom-call | tf_op jit(solution)/shard_map/jit(cholesky)/cholesky | solution.py:14
  530.5 0.6 compare_reduce_fusion
  531.1 0.7 compare_reduce_fusion.2
  534.5 8.5 %while.1 = (s32[]{:T(128)}, f32[512,512]{1,0:T(8,128)S(1)}, s32[4,2]{0,1:T(2,128)S(1)}, f32[4,128,128]{2,1,0:T(8,128)S(1)}, s32[]{:T(128)}) while((s32[]{:T(128)}, f32[512,512]{1,0:T(8,128)S(1)}, s32[4,2]{0,1:T(2,128)S(1)}, f32[4,128,128]{2,1,0:T(8,128)S(1)}, s32[]{:T(128)}) %tuple.31), condition=%wide.while_cond, body=%wide.while_body.sunk | while | flops 2 | bytes 131181 | solution.py:15
  535.2 1.4 bitcast_dynamic-update-slice_fusion.2
  537.3 1.4 bitcast_dynamic-update-slice_fusion.2
  539.4 1.4 bitcast_dynamic-update-slice_fusion.2
  541.5 1.4 bitcast_dynamic-update-slice_fusion.2
  543.0 39.3 %custom-call.34 = f32[4,128,128]{1,2,0:T(8,128)S(1)} custom-call(f32[4,128,128]{2,1,0:T(8,128)S(1)} %get-tuple-element.10), custom_call_target="InvertDiagBlocksLowerTriangular" | custom-call | tf_op jit(solution)/shard_map/jit(_solve_triangular)/triangular_solve | solution.py:15
  582.3 2.4 fusion.19
  584.8 2.6 fusion.30
  587.4 1.1 fusion.18
  588.6 4.9 fusion.9
  593.5 1.1 fusion.17
  594.6 7.2 fusion.3
  601.8 1.1 fusion.16
  603.0 1.0 copy-done.6
  603.9 56.3 %fusion = f32[2048,512]{1,0:T(8,128)} fusion(f32[2048,2048]{1,0:T(8,128)} %param.5, bf16[2048,2048]{1,0:T(8,128)(2,1)S(1)} %bitcast.51, f32[128,2048]{1,0:T(8,128)S(1)} %fusion.16, f32[128,2048]{1,0:T(8,128)S(1)} %fusion.17, f32[128,2048]{1,0:T(8,128)S(1)} %fusion.18, f32[128,2048]{1,0:T(8,128)S(1)} %fusion.19), kind=kOutput, calls=%fused_computation.5 | convolution fusion | flops 25781338112 | bytes 33554432 | tf_op jit(solution)/shard_map/dot_general | solution.py:30
  660.3 45.2 %reduce-scatter.2.cloned.1.call-done = f32[512,512]{1,0:T(8,128)} async-done(((f32[2048,512]{1,0:T(8,128)}), f32[512,512]{1,0:T(8,128)}) %reduce-scatter.2.cloned.1.call-update) | async-done | bytes 1048592 | tf_op jit(solution)/shard_map/reduce_scatter | solution.py:29
  705.5 1.3 multiply_reduce_fusion
  706.8 39.2 %psum.15 = f32[512]{0:T(512)S(1)} all-reduce(f32[512]{0:T(512)S(1)} %multiply_reduce_fusion), channel_id=1, replica_groups=mesh['row'=4,'col'=8] {'row','col'}, use_global_device_ids=true, to_apply=%region_11.12 | all-reduce | flops 512 | bytes 4096 | tf_op jit(solution)/shard_map/psum | solution.py:32
  746.1 2.1 divide_convert_fusion
  748.2 23.4 %all-gather.2.cloned.1.call-done = bf16[2048,512]{1,0:T(8,128)(2,1)} async-done(((bf16[512,512]{1,0:T(8,128)(2,1)}), bf16[2048,512]{1,0:T(8,128)(2,1)}) %all-gather.2.cloned.1.call-update) | async-done | bytes 2097168 | tf_op jit(solution)/shard_map/all_gather | solution.py:35
  771.7 35.6 %multiply_subtract_fusion = f32[2048,2048]{1,0:T(8,128)} fusion(bf16[2048,512]{1,0:T(8,128)(2,1)} %all-gather.2.cloned.1.call-done, f32[2048,2048]{1,0:T(8,128)} %param.5, bf16[2048,2048]{1,0:T(8,128)(2,1)} %param.6, f32[512]{0:T(512)S(1)} %add_sqrt_fusion, f32[128,2048]{1,0:T(8,128)} %copy-done.6, f32[128,2048]{1,0:T(8,128)S(1)} %fusion.17, ...), kind=kOutput, calls=%fused_computation.2 | convolution fusion | flops 25790775296 | bytes 48236544 | tf_op jit(solution)/shard_map/dot_general | solution.py:37
  807.3 32.0 %subtract_convert_fusion = bf16[2048,2048]{1,0:T(8,128)(2,1)} fusion(bf16[2048,2048]{1,0:T(8,128)(2,1)} %param.4, bf16[2048,512]{1,0:T(8,128)(2,1)} %all-gather.2.cloned.1.call-done, f32[128,2048]{1,0:T(8,128)} %copy-done.6, f32[128,2048]{1,0:T(8,128)} %copy-done.4, f32[128,2048]{1,0:T(8,128)} %copy-done.2, f32[128,2048]{1,0:T(8,128)S(1)} %fusion.19), kind=kOutput, calls=%fused_computation.3 | convolution fusion | flops 25789726720 | bytes 23068672 | tf_op jit(solution)/shard_map/dot_general | solution.py:40
  839.4 1.3 copy.27
  (52 shorter events, 5.4 us)
Async XLA Ops:
  7.2 1.6 copy-start
  7.2 440.5 %all-reduce.3.cloned.1.call-start = ((), (), s32[]{:S(2)}) async-start(), calls=%async_computation.1 | async-start | bytes 2097152 | tf_op jit(solution)/shard_map/psum | solution.py:27
  25.4 93.6 %collective-permute-start = (f32[2048,512]{1,0:T(8,128)S(1)}, f32[2048,512]{1,0:T(8,128)S(1)}, u32[]{:S(2)}, u32[]{:S(2)}) collective-permute-start(f32[2048,512]{1,0:T(8,128)S(1)} %fusion.1), channel_id=1, source_target_pairs={{0,1},{1,0},{2,3},{3,2},{4,5},{5,4},{6,7},{7,6},{8,9},{9,8},{10,11... | collective-permute-start | bytes 12582920 | tf_op jit(solution)/shard_map/ppermute | solution.py:24
  120.0 91.8 %collective-permute-start.1 = (f32[2048,512]{1,0:T(8,128)S(1)}, f32[2048,512]{1,0:T(8,128)S(1)}, u32[]{:S(2)}, u32[]{:S(2)}) collective-permute-start(f32[2048,512]{1,0:T(8,128)S(1)} %add.66), channel_id=1, source_target_pairs={{0,2},{1,3},{2,0},{3,1},{4,6},{5,7},{6,4},{7,5},{8,10},{9,11},{10,... | collective-permute-start | bytes 12582920 | tf_op jit(solution)/shard_map/ppermute | solution.py:24
  214.8 182.0 %collective-permute-start.2 = (f32[2048,512]{1,0:T(8,128)}, f32[2048,512]{1,0:T(8,128)}, u32[]{:S(2)}, u32[]{:S(2)}) collective-permute-start(f32[2048,512]{1,0:T(8,128)} %add.67), channel_id=1, source_target_pairs={{0,4},{1,5},{2,6},{3,7},{4,0},{5,1},{6,2},{7,3},{8,12},{9,13},{10,... | collective-permute-start | bytes 12582920 | tf_op jit(solution)/shard_map/ppermute | solution.py:24
  410.4 295.1 %reduce-scatter.2.cloned.1.call-start = ((), (), s32[]{:S(2)}) async-start(), calls=%async_computation.2 | async-start | bytes 5242880 | tf_op jit(solution)/shard_map/reduce_scatter | solution.py:29
  543.0 39.3 %copy-start.7 = (f32[512,512]{1,0:T(8,128)}, f32[512,512]{1,0:T(8,128)S(1)}, u32[]{:S(2)}) copy-start(f32[512,512]{1,0:T(8,128)S(1)} %get-tuple-element.99) | copy-start | bytes 3145732
  582.3 5.1 copy-start.3
  587.4 16.5 %slice-start = ((s8[8388608]{0:T(1024)(128)(4,1)}), s8[4194304]{0:T(1024)(128)(4,1)S(1)}, s32[]{:S(2)}) async-start(s8[8388608]{0:T(1024)(128)(4,1)} %bitcast.50), calls=%async_computation.4 | async-start | bytes 8388608
  588.6 183.1 %copy-start.2 = (f32[128,2048]{1,0:T(8,128)}, f32[128,2048]{1,0:T(8,128)S(1)}, u32[]{:S(2)}) copy-start(f32[128,2048]{1,0:T(8,128)S(1)} %fusion.18) | copy-start | bytes 3145732
  593.5 10.4 %slice-start.1 = ((s8[8388608]{0:T(1024)(128)(4,1)}), s8[4194304]{0:T(1024)(128)(4,1)S(1)}, s32[]{:S(2)}) async-start(s8[8388608]{0:T(1024)(128)(4,1)} %bitcast.50), calls=%async_computation.5 | async-start | bytes 8388608
  594.6 177.1 %copy-start.4 = (f32[128,2048]{1,0:T(8,128)}, f32[128,2048]{1,0:T(8,128)S(1)}, u32[]{:S(2)}) copy-start(f32[128,2048]{1,0:T(8,128)S(1)} %fusion.17) | copy-start | bytes 3145732
  602.9 1.0 copy-start.6
  660.3 111.4 %all-gather.2.cloned.1.call-start = ((), (), s32[]{:S(2)}) async-start(), calls=%async_computation.3 | async-start | bytes 2621440 | tf_op jit(solution)/shard_map/all_gather | solution.py:35
  807.3 32.1 %copy-start.5 = (bf16[2048,512]{1,0:T(8,128)(2,1)S(1)}, bf16[2048,512]{1,0:T(8,128)(2,1)}, u32[]{:S(2)}) copy-start(bf16[2048,512]{1,0:T(8,128)(2,1)} %all-gather.2.cloned.1.call-done) | copy-start | bytes 6291460
  807.3 33.4 %copy-start.1 = (bf16[2048,512]{1,0:T(8,128)(2,1)S(1)}, bf16[2048,512]{1,0:T(8,128)(2,1)}, u32[]{:S(2)}) copy-start(bf16[2048,512]{1,0:T(8,128)(2,1)} %param.7) | copy-start | bytes 6291460
Sparse Core Ops, SparseCore 0:
  410.5 37.1 all-reduce.2
  660.4 45.0 reduce-scatter.1
  748.4 23.2 all-gather.1
